TPU v7x, 32 devices: a whole 2x2x4 slice. The times are simulated.
32 devices in a mesh: rep: 2 (over x), fsdp: 16 (over z, y, core).
Axes of the slice: x: 2, y: 2, z: 4, core: 2. Of those that a mesh axis runs over, the one named last changes fastest.
Arguments:
- input_short: bfloat16 [128, 128, 768], P(('rep', 'fsdp')), may hold values from -6 to 6
- input_long: bfloat16 [64, 256, 768], P(('rep', 'fsdp')), may hold values from -6 to 6
- steps_short: int32 [128], P(('rep', 'fsdp')), may hold values from 0 to 999
- steps_long: int32 [64], P(('rep', 'fsdp')), may hold values from 0 to 999
- upstream_short: bfloat16 [128, 128, 768], P(('rep', 'fsdp')), may hold values from -6 to 6
- upstream_long: bfloat16 [64, 256, 768], P(('rep', 'fsdp')), may hold values from -6 to 6
- step_table: float32 [1000, 768], P(None, 'fsdp'), may hold values from -3 to 3
- attn_gain: float32 [768], P('fsdp'), may hold values from 0.5 to 1.5
- attn_shift: float32 [768], P('fsdp'), may hold values from -2 to 2
- qkv_weight: float32 [768, 2304], P('fsdp'), may hold values from -0.21875 to 0.21875
- query_bias: float32 [768], P('fsdp'), may hold values from -2 to 2
- value_bias: float32 [768], P('fsdp'), may hold values from -2 to 2
- out_weight: float32 [768, 768], P('fsdp'), may hold values from -0.625 to 0.625
- out_bias: float32 [768], P('fsdp'), may hold values from -2 to 2
- ffn_gain: float32 [768], P('fsdp'), may hold values from 0.5 to 1.5
- ffn_shift: float32 [768], P('fsdp'), may hold values from -2 to 2
- up_weight: float32 [768, 3072], P('fsdp'), may hold values from -0.21875 to 0.21875
- up_bias: float32 [3072], P('fsdp'), may hold values from -2 to 2
- down_weight: float32 [3072, 768], P('fsdp'), may hold values from -0.15625 to 0.15625
- down_bias: float32 [768], P('fsdp'), may hold values from -2 to 2
Outputs:
- output_short: bfloat16 [128, 128, 768], P(('rep', 'fsdp'))
- output_long: bfloat16 [64, 256, 768], P(('rep', 'fsdp'))
- input_grad_short: bfloat16 [128, 128, 768], P(('rep', 'fsdp'))
- input_grad_long: bfloat16 [64, 256, 768], P(('rep', 'fsdp'))
- table_grad: float32 [1000, 768], P(None, 'fsdp')
- attn_gain_grad: float32 [768], P('fsdp')
- attn_shift_grad: float32 [768], P('fsdp')
- qkv_weight_grad: float32 [768, 2304], P('fsdp')
- query_bias_grad: float32 [768], P('fsdp')
- value_bias_grad: float32 [768], P('fsdp')
- out_weight_grad: float32 [768, 768], P('fsdp')
- out_bias_grad: float32 [768], P('fsdp')
- ffn_gain_grad: float32 [768], P('fsdp')
- ffn_shift_grad: float32 [768], P('fsdp')
- up_weight_grad: float32 [768, 3072], P('fsdp')
- up_bias_grad: float32 [3072], P('fsdp')
- down_weight_grad: float32 [3072, 768], P('fsdp')
- down_bias_grad: float32 [768], P('fsdp')
All inputs are finite; a program needn't handle non-finite values.
Results may differ from a plain program's by a relative error of at most 0.014.
Values may be sent and summed in bfloat16 or wider, within the bound.
No kernel may reach another device: no remote copies, remote signals or barrier semaphores. Data moves between devices by JAX's collectives and lax.ppermute only.
A program may use at most 192 MiB of HBM per device.

v0:
```python
from functools import partial
import jax
import jax.numpy as jnp
from jax import lax
from jax.sharding import PartitionSpec as P

HEAD_DIM = 64
bfloat = jnp.bfloat16
single = jnp.float32
precise = lax.Precision.HIGHEST


def across_rows(left, right):
    return lax.dot_general(
        left, right, (((0,), (0,)), ((), ())), preferred_element_type=jnp.float32
    )


def against(left, right):
    return lax.dot_general(
        left, right, (((1,), (1,)), ((), ())), preferred_element_type=jnp.float32
    )


def normalize(hidden, gain, shift):
    centre = hidden - jnp.mean(hidden, axis=-1, keepdims=True)
    factor = lax.rsqrt(jnp.mean(centre * centre, axis=-1, keepdims=True) + 1e-05)
    scaled = centre * factor
    return (scaled * gain + shift, scaled, factor)


def norm_back(upper, scaled, factor, gain):
    inner = upper * gain
    lower = factor * (
        inner
        - jnp.mean(inner, axis=-1, keepdims=True)
        - scaled * jnp.mean(inner * scaled, axis=-1, keepdims=True)
    )
    return (lower, jnp.sum(upper * scaled, axis=0), jnp.sum(upper, axis=0))


def forward_group(rows, steps, weights):
    (
        table,
        attn_gain,
        attn_shift,
        qkv_weight,
        query_bias,
        value_bias,
        out_weight,
        out_bias,
        ffn_gain,
        ffn_shift,
        up_weight,
        up_bias,
        down_weight,
        down_bias,
    ) = weights
    count, length, width = rows.shape
    heads = width // HEAD_DIM
    scale = HEAD_DIM ** (-0.5)
    start = (rows.astype(single) + table[steps].astype(single)[:, None, :]).reshape(
        count * length, width
    )
    normed_one, scaled_one, factor_one = normalize(
        start, attn_gain.astype(single), attn_shift.astype(single)
    )
    first = normed_one.astype(bfloat)
    joined_bias = jnp.concatenate([query_bias, jnp.zeros_like(query_bias), value_bias]).astype(
        single
    )
    projected = (jnp.dot(first, qkv_weight, preferred_element_type=single) + joined_bias).astype(
        bfloat
    )
    shaped = projected.reshape(count, length, 3, heads, HEAD_DIM)
    query = shaped[:, :, 0]
    keys = shaped[:, :, 1]
    values = shaped[:, :, 2]
    scores = jnp.einsum("sqhe,skhe->shqk", query, keys, preferred_element_type=single) * scale
    summit = jnp.max(scores, axis=-1, keepdims=True)
    expo = jnp.exp(scores - summit)
    totals = jnp.sum(expo, axis=-1, keepdims=True)
    probs_low = (expo / totals).astype(bfloat)
    logsum = summit + jnp.log(totals)
    mixed = jnp.einsum("shqk,skhe->sqhe", probs_low, values, preferred_element_type=single)
    mixed = mixed.reshape(count * length, width).astype(bfloat)
    middle = (
        start + jnp.dot(mixed, out_weight, preferred_element_type=single) + out_bias.astype(single)
    )
    normed_two, scaled_two, factor_two = normalize(
        middle, ffn_gain.astype(single), ffn_shift.astype(single)
    )
    second = normed_two.astype(bfloat)
    hidden = jnp.dot(second, up_weight, preferred_element_type=single) + up_bias.astype(single)
    active = jax.nn.gelu(hidden, approximate=True).astype(bfloat)
    result = (
        middle
        + jnp.dot(active, down_weight, preferred_element_type=single)
        + down_bias.astype(single)
    )
    saved = (
        scaled_one,
        factor_one,
        first,
        query,
        keys,
        values,
        logsum,
        mixed,
        scaled_two,
        factor_two,
        second,
        hidden,
        active,
    )
    return (result.reshape(count, length, width).astype(bfloat), saved)


def backward_group(upstream, steps, weights, saved):
    (
        table,
        attn_gain,
        attn_shift,
        qkv_weight,
        query_bias,
        value_bias,
        out_weight,
        out_bias,
        ffn_gain,
        ffn_shift,
        up_weight,
        up_bias,
        down_weight,
        down_bias,
    ) = weights
    (
        scaled_one,
        factor_one,
        first,
        query,
        keys,
        values,
        logsum,
        mixed,
        scaled_two,
        factor_two,
        second,
        hidden,
        active,
    ) = saved
    count, length, width = upstream.shape
    heads = width // HEAD_DIM
    scale = HEAD_DIM ** (-0.5)
    flat = upstream.reshape(count * length, width)
    grad_rows = flat.astype(single)
    down_weight_grad = across_rows(active, flat)
    down_bias_grad = jnp.sum(grad_rows, axis=0)
    _, gelu_pull = jax.vjp(partial(jax.nn.gelu, approximate=True), hidden)
    hidden_grad = gelu_pull(against(flat, down_weight))[0].astype(bfloat)
    up_weight_grad = across_rows(second, hidden_grad)
    up_bias_grad = jnp.sum(hidden_grad.astype(single), axis=0)
    middle_part, ffn_gain_grad, ffn_shift_grad = norm_back(
        against(hidden_grad, up_weight), scaled_two, factor_two, ffn_gain.astype(single)
    )
    middle_grad = grad_rows + middle_part
    branch_grad = middle_grad.astype(bfloat)
    out_weight_grad = across_rows(mixed, branch_grad)
    out_bias_grad = jnp.sum(branch_grad.astype(single), axis=0)
    mixed_grad = (
        against(branch_grad, out_weight).astype(bfloat).reshape(count, length, heads, HEAD_DIM)
    )
    scores = jnp.einsum("sqhe,skhe->shqk", query, keys, preferred_element_type=single) * scale
    probs = jnp.exp(scores - logsum)
    probs_grad = jnp.einsum("sqhe,skhe->shqk", mixed_grad, values, preferred_element_type=single)
    values_grad = jnp.einsum(
        "shqk,sqhe->skhe", probs.astype(bfloat), mixed_grad, preferred_element_type=single
    )
    scores_grad = (
        probs * (probs_grad - jnp.sum(probs_grad * probs, axis=-1, keepdims=True))
    ).astype(bfloat)
    query_grad = (
        jnp.einsum("shqk,skhe->sqhe", scores_grad, keys, preferred_element_type=single) * scale
    )
    keys_grad = (
        jnp.einsum("shqk,sqhe->skhe", scores_grad, query, preferred_element_type=single) * scale
    )
    projected_grad = jnp.stack([query_grad, keys_grad, values_grad], axis=2)
    projected_grad = projected_grad.reshape(count * length, 3 * width).astype(bfloat)
    qkv_weight_grad = across_rows(first, projected_grad)
    column_sums = jnp.sum(projected_grad.astype(single), axis=0)
    query_bias_grad = column_sums[:width]
    value_bias_grad = column_sums[2 * width :]
    start_part, attn_gain_grad, attn_shift_grad = norm_back(
        against(projected_grad, qkv_weight), scaled_one, factor_one, attn_gain.astype(single)
    )
    start_grad = middle_grad + start_part
    sequence_sums = jnp.sum(start_grad.reshape(count, length, width), axis=1)
    selector = (steps[:, None] == jnp.arange(table.shape[0], dtype=jnp.int32)[None, :]).astype(
        single
    )
    table_grad = lax.dot_general(
        selector,
        sequence_sums,
        (((0,), (0,)), ((), ())),
        precision=precise,
        preferred_element_type=single,
    )
    grads = (
        table_grad,
        attn_gain_grad,
        attn_shift_grad,
        qkv_weight_grad,
        query_bias_grad,
        value_bias_grad,
        out_weight_grad,
        out_bias_grad,
        ffn_gain_grad,
        ffn_shift_grad,
        up_weight_grad,
        up_bias_grad,
        down_weight_grad,
        down_bias_grad,
    )
    return (start_grad.reshape(count, length, width).astype(bfloat), grads)


def shards(
    input_short,
    input_long,
    steps_short,
    steps_long,
    upstream_short,
    upstream_long,
    step_table,
    attn_gain,
    attn_shift,
    qkv_weight,
    query_bias,
    value_bias,
    out_weight,
    out_bias,
    ffn_gain,
    ffn_shift,
    up_weight,
    up_bias,
    down_weight,
    down_bias,
):
    masters = (
        step_table,
        attn_gain,
        attn_shift,
        qkv_weight,
        query_bias,
        value_bias,
        out_weight,
        out_bias,
        ffn_gain,
        ffn_shift,
        up_weight,
        up_bias,
        down_weight,
        down_bias,
    )
    copies = tuple((each.astype(bfloat) for each in masters))
    gathered = (
        lax.all_gather(copies[0], "fsdp", axis=1, tiled=True),
        lax.all_gather(copies[1], "fsdp", axis=0, tiled=True),
        lax.all_gather(copies[2], "fsdp", axis=0, tiled=True),
        lax.all_gather(copies[3], "fsdp", axis=0, tiled=True),
        lax.all_gather(copies[4], "fsdp", axis=0, tiled=True),
        lax.all_gather(copies[5], "fsdp", axis=0, tiled=True),
        lax.all_gather(copies[6], "fsdp", axis=0, tiled=True),
        lax.all_gather(copies[7], "fsdp", axis=0, tiled=True),
        lax.all_gather(copies[8], "fsdp", axis=0, tiled=True),
        lax.all_gather(copies[9], "fsdp", axis=0, tiled=True),
        lax.all_gather(copies[10], "fsdp", axis=0, tiled=True),
        lax.all_gather(copies[11], "fsdp", axis=0, tiled=True),
        lax.all_gather(copies[12], "fsdp", axis=0, tiled=True),
        lax.all_gather(copies[13], "fsdp", axis=0, tiled=True),
    )
    output_short, saved_short = forward_group(input_short, steps_short, gathered)
    output_long, saved_long = forward_group(input_long, steps_long, gathered)
    reused = (
        lax.all_gather(copies[0], "fsdp", axis=1, tiled=True),
        lax.all_gather(copies[1], "fsdp", axis=0, tiled=True),
        lax.all_gather(copies[2], "fsdp", axis=0, tiled=True),
        lax.all_gather(copies[3], "fsdp", axis=0, tiled=True),
        lax.all_gather(copies[4], "fsdp", axis=0, tiled=True),
        lax.all_gather(copies[5], "fsdp", axis=0, tiled=True),
        lax.all_gather(copies[6], "fsdp", axis=0, tiled=True),
        lax.all_gather(copies[7], "fsdp", axis=0, tiled=True),
        lax.all_gather(copies[8], "fsdp", axis=0, tiled=True),
        lax.all_gather(copies[9], "fsdp", axis=0, tiled=True),
        lax.all_gather(copies[10], "fsdp", axis=0, tiled=True),
        lax.all_gather(copies[11], "fsdp", axis=0, tiled=True),
        lax.all_gather(copies[12], "fsdp", axis=0, tiled=True),
        lax.all_gather(copies[13], "fsdp", axis=0, tiled=True),
    )
    grad_short, grads_short = backward_group(upstream_short, steps_short, reused, saved_short)
    grad_long, grads_long = backward_group(upstream_long, steps_long, reused, saved_long)
    totals = tuple((left + right for left, right in zip(grads_short, grads_long)))
    shares = (
        lax.psum_scatter(totals[0], "fsdp", scatter_dimension=1, tiled=True),
        lax.psum_scatter(totals[1], "fsdp", scatter_dimension=0, tiled=True),
        lax.psum_scatter(totals[2], "fsdp", scatter_dimension=0, tiled=True),
        lax.psum_scatter(totals[3], "fsdp", scatter_dimension=0, tiled=True),
        lax.psum_scatter(totals[4], "fsdp", scatter_dimension=0, tiled=True),
        lax.psum_scatter(totals[5], "fsdp", scatter_dimension=0, tiled=True),
        lax.psum_scatter(totals[6], "fsdp", scatter_dimension=0, tiled=True),
        lax.psum_scatter(totals[7], "fsdp", scatter_dimension=0, tiled=True),
        lax.psum_scatter(totals[8], "fsdp", scatter_dimension=0, tiled=True),
        lax.psum_scatter(totals[9], "fsdp", scatter_dimension=0, tiled=True),
        lax.psum_scatter(totals[10], "fsdp", scatter_dimension=0, tiled=True),
        lax.psum_scatter(totals[11], "fsdp", scatter_dimension=0, tiled=True),
        lax.psum_scatter(totals[12], "fsdp", scatter_dimension=0, tiled=True),
        lax.psum_scatter(totals[13], "fsdp", scatter_dimension=0, tiled=True),
    )
    reduced = (
        lax.psum(shares[0].astype(jnp.bfloat16), "rep").astype(jnp.float32),
        lax.psum(shares[1].astype(jnp.bfloat16), "rep").astype(jnp.float32),
        lax.psum(shares[2].astype(jnp.bfloat16), "rep").astype(jnp.float32),
        lax.psum(shares[3].astype(jnp.bfloat16), "rep").astype(jnp.float32),
        lax.psum(shares[4].astype(jnp.bfloat16), "rep").astype(jnp.float32),
        lax.psum(shares[5].astype(jnp.bfloat16), "rep").astype(jnp.float32),
        lax.psum(shares[6].astype(jnp.bfloat16), "rep").astype(jnp.float32),
        lax.psum(shares[7].astype(jnp.bfloat16), "rep").astype(jnp.float32),
        lax.psum(shares[8].astype(jnp.bfloat16), "rep").astype(jnp.float32),
        lax.psum(shares[9].astype(jnp.bfloat16), "rep").astype(jnp.float32),
        lax.psum(shares[10].astype(jnp.bfloat16), "rep").astype(jnp.float32),
        lax.psum(shares[11].astype(jnp.bfloat16), "rep").astype(jnp.float32),
        lax.psum(shares[12].astype(jnp.bfloat16), "rep").astype(jnp.float32),
        lax.psum(shares[13].astype(jnp.bfloat16), "rep").astype(jnp.float32),
    )
    return (output_short, output_long, grad_short, grad_long) + tuple(reduced)


def solution(mesh):
    in_specs = (
        P(("rep", "fsdp"), None, None),
        P(("rep", "fsdp"), None, None),
        P(("rep", "fsdp")),
        P(("rep", "fsdp")),
        P(("rep", "fsdp"), None, None),
        P(("rep", "fsdp"), None, None),
        P(None, "fsdp"),
        P("fsdp"),
        P("fsdp"),
        P("fsdp", None),
        P("fsdp"),
        P("fsdp"),
        P("fsdp", None),
        P("fsdp"),
        P("fsdp"),
        P("fsdp"),
        P("fsdp", None),
        P("fsdp"),
        P("fsdp", None),
        P("fsdp"),
    )
    out_specs = (
        P(("rep", "fsdp"), None, None),
        P(("rep", "fsdp"), None, None),
        P(("rep", "fsdp"), None, None),
        P(("rep", "fsdp"), None, None),
        P(None, "fsdp"),
        P("fsdp"),
        P("fsdp"),
        P("fsdp", None),
        P("fsdp"),
        P("fsdp"),
        P("fsdp", None),
        P("fsdp"),
        P("fsdp"),
        P("fsdp"),
        P("fsdp", None),
        P("fsdp"),
        P("fsdp", None),
        P("fsdp"),
    )
    return jax.shard_map(shards, mesh=mesh, in_specs=in_specs, out_specs=out_specs, check_vma=False)
```

profile of v0, /device:TPU:0, one launch (start us, length us, event | category | flops | bytes accessed | tf_op | source)
XLA Modules:
  0.0 840.2 jit_solution(3104983572715529575)
XLA Ops:
  19.3 63.8 %all-reduce.19 = (bf16[768]{0:T(1024)(128)(2,1)S(1)}, bf16[768]{0:T(1024)(128)(2,1)S(1)}, bf16[768]{0:T(1024)(128)(2,1)S(1)}, bf16[768]{0:T(1024)(128)(2,1)S(1)}...) all-reduce(bf16[768]{0:T(1024)(128)(2,1)S(1)} %dynamic-update-slice, ...), channel_id=1, replica_groups=mesh['rep'=2,'fsdp'=16] {'fsdp'}, use_global_device_ids=true, to_apply=%add.4 | all-reduce | flops 9216 | bytes 36864
  83.2 2.0 copy.84
  92.1 10.4 %all-gather.8.cloned.1.call-done = bf16[768,2304]{1,0:T(8,128)(2,1)} async-done(((bf16[48,2304]{1,0:T(8,128)(2,1)}), bf16[768,2304]{1,0:T(8,128)(2,1)}) %all-gather.8.cloned.1.call-update) | async-done | bytes 3538960 | tf_op jit(solution)/shard_map/all_gather | solution.py:270
  102.4 5.4 fusion.16
  107.9 2.8 copy.92
  110.7 2.2 reshape.319
  112.9 4.0 fusion.15
  116.9 2.5 copy.85
  119.4 4.2 reshape.317
  128.8 2.2 fusion.88
  138.0 4.7 all-gather.10.cloned.1.call-done
  142.7 3.1 fusion.91
  148.6 49.2 %all-gather.12.cloned.1.call-done = bf16[768,3072]{1,0:T(8,128)(2,1)} async-done(((bf16[48,3072]{1,0:T(8,128)(2,1)}), bf16[768,3072]{1,0:T(8,128)(2,1)}) %all-gather.12.cloned.1.call-update) | async-done | bytes 4718608 | tf_op jit(solution)/shard_map/all_gather | solution.py:277
  197.8 8.2 fusion.83
  206.0 4.9 fusion.84
  211.0 41.5 %all-gather.14.cloned.1.call-done = bf16[3072,768]{1,0:T(8,128)(2,1)} async-done(((bf16[192,768]{1,0:T(8,128)(2,1)}), bf16[3072,768]{1,0:T(8,128)(2,1)}) %all-gather.14.cloned.1.call-update) | async-done | bytes 4718608 | tf_op jit(solution)/shard_map/all_gather | solution.py:279
  252.5 7.9 fusion.93
  260.4 13.6 %convert_reduce_fusion = (f32[3072]{0:T(1024)S(1)}, bf16[512,3072]{1,0:T(8,128)(2,1)S(1)}, f32[3072]{0:T(1024)S(1)}, bf16[512,3072]{1,0:T(8,128)(2,1)S(1)}) fusion(f32[512,3072]{1,0:T(8,128)} %fusion.84, f32[3072]{0:T(1024)S(1)} %convert_element_type.381, f32[512,3072]{1,0:T(8,128)} %fusion.93, f32[512,3072]{1,0:T(8,128)} %fusion.83, ...), kind=kOutput, calls=%fused_computation.20 | convolution fusion | flops 2488264704 | bytes 30707712 | tf_op jit(solution)/shard_map/dot_general | solution.py:20
  274.1 7.7 multiply_reduce_fusion.4
  281.9 7.0 convert_reduce_fusion.6
  290.1 2.2 fusion.52
  294.0 2.3 copy.98
  296.3 2.8 reshape.321
  299.2 3.3 fusion.43
  304.8 2.1 multiply_bitcast_fusion.2
  310.9 2.4 reshape.324
  313.2 5.1 multiply_reduce_fusion
  323.6 2.2 convolution_add_fusion.6
  329.1 2.2 copy.104
  331.3 5.1 fusion.40
  336.8 2.5 copy.111
  341.4 2.1 fusion.26
  343.5 3.8 multiply_reduce_fusion.6
  351.9 3.2 convolution_add_fusion.5
  356.3 3.8 fusion.24
  360.1 4.9 convolution_add_fusion
  366.2 5.9 fusion.85
  372.1 10.2 %convolution_add_fusion.1 = f32[3072,768]{1,0:T(8,128)} fusion(f32[3072,768]{1,0:T(8,128)S(1)} %fusion.85, bf16[512,768]{1,0:T(8,128)(2,1)S(1)} %bitcast.216, f32[512,3072]{1,0:T(8,128)} %fusion.84, f32[3072]{0:T(1024)S(1)} %convert_element_type.381), kind=kOutput, calls=%fused_computation.31 | convolution fusion | flops 2434007040 | bytes 25964544 | tf_op jit(solution)/shard_map/dot_general | solution.py:14
  383.7 5.0 fusion.82
  388.7 5.7 convolution_add_fusion.2
  398.7 59.9 %all-reduce.18 = (bf16[768]{0:T(1024)(128)(2,1)S(1)}, bf16[768]{0:T(1024)(128)(2,1)S(1)}, bf16[768]{0:T(1024)(128)(2,1)S(1)}, bf16[768]{0:T(1024)(128)(2,1)S(1)}...) all-reduce(f32[768]{0:T(1024)S(1)} %add.357, ...), channel_id=3, replica_groups=mesh['rep'=2,'fsdp'=16] {'fsdp'}, use_global_device_ids=true, to_apply=%region_28.0.clone | all-reduce | flops 9216 | bytes 55296
  459.3 5.1 all-reduce.20
  469.1 9.9 %add_convert_fusion.5 = bf16[512,768]{1,0:T(8,128)(2,1)} fusion(f32[512,768]{1,0:T(8,128)S(1)} %copy-done.32, bf16[3072,768]{1,0:T(8,128)(2,1)} %all-gather.14.cloned.1.call-done, f32[768]{0:T(1024)S(1)} %convert_element_type.385, f32[512,3072]{1,0:T(8,128)} %fusion.83, f32[3072]{0:T(1024)S(1)} %convert_element_type.381), kind=kOutput, calls=%fused_computation.103 | convolution fusion | flops 2432827392 | bytes 13384704 | tf_op jit(solution)/shard_map/dot_general | solution.py:98
  482.2 68.6 %reduce-scatter.8.cloned.1.call-done = f32[48,2304]{1,0:T(8,128)} async-done(((f32[768,2304]{1,0:T(8,128)}), f32[48,2304]{1,0:T(8,128)}) %reduce-scatter.8.cloned.1.call-update) | async-done | bytes 442384 | tf_op jit(solution)/shard_map/reduce_scatter | solution.py:307
  552.6 113.3 %reduce-scatter.14.cloned.1.call-done = f32[192,768]{1,0:T(8,128)} async-done(((f32[3072,768]{1,0:T(8,128)}), f32[192,768]{1,0:T(8,128)}) %reduce-scatter.14.cloned.1.call-update) | async-done | bytes 589840 | tf_op jit(solution)/shard_map/reduce_scatter | solution.py:316
  667.7 113.8 %reduce-scatter.12.cloned.1.call-done = f32[48,3072]{1,0:T(8,128)} async-done(((f32[768,3072]{1,0:T(8,128)}), f32[48,3072]{1,0:T(8,128)}) %reduce-scatter.12.cloned.1.call-update) | async-done | bytes 589840 | tf_op jit(solution)/shard_map/reduce_scatter | solution.py:314
  783.3 9.0 %add_convert_fusion.2 = bf16[512,768]{1,0:T(8,128)(2,1)} fusion(f32[512,768]{1,0:T(8,128)S(1)} %copy-done.13, bf16[3072,768]{1,0:T(8,128)(2,1)} %all-gather.14.cloned.1.call-done, f32[768]{0:T(1024)S(1)} %convert_element_type.385, f32[512,3072]{1,0:T(8,128)} %fusion.84, f32[3072]{0:T(1024)S(1)} %convert_element_type.381), kind=kOutput, calls=%fused_computation.97 | convolution fusion | flops 2432827392 | bytes 13384704 | tf_op jit(solution)/shard_map/dot_general | solution.py:98
  792.3 32.6 %all-reduce.24.cloned.1.call-done = (bf16[1000,48]{0,1:T(8,128)(2,1)}, bf16[48,2304]{1,0:T(8,128)(2,1)}, bf16[48,768]{1,0:T(8,128)(2,1)}, bf16[48,3072]{1,0:T(8,128)(2,1)}, bf16[192,768]{1,0:T(8,128)(2,1)}) async-done(((bf16[1000,48]{0,1:T(8,128)(2,1)}, bf16[48,2304]{1,0:T(8,128)(2,1)}, bf16[48,768]{1,0:T(8,128)(2,1)}, bf16[48,3072]{1,0:T(8,128)(2,1)}, bf16[192,768]{1,0:T(8,128)(2,1)}), ...) | async-done | bytes 980752 | tf_op jit(solution)/shard_map/psum | solution.py:320
  (317 shorter events, 85.5 us)
Async XLA Ops:
  7.2 8.0 copy-start.52
  7.2 7.2 copy-start.50
  7.2 9.9 %copy-start.62 = (f32[48]{0:T(128)S(1)}, f32[48]{0:T(128)}, u32[]{:S(2)}) copy-start(f32[48]{0:T(128)} %param.27) | copy-start | bytes 580
  7.2 9.9 %copy-start.63 = (f32[48]{0:T(128)S(1)}, f32[48]{0:T(128)}, u32[]{:S(2)}) copy-start(f32[48]{0:T(128)} %param.28) | copy-start | bytes 580
  7.2 9.9 %copy-start.64 = (f32[48]{0:T(128)S(1)}, f32[48]{0:T(128)}, u32[]{:S(2)}) copy-start(f32[48]{0:T(128)} %param.30) | copy-start | bytes 580
  7.2 9.9 %copy-start.65 = (f32[48]{0:T(128)S(1)}, f32[48]{0:T(128)}, u32[]{:S(2)}) copy-start(f32[48]{0:T(128)} %param.31) | copy-start | bytes 580
  7.3 9.9 %copy-start.66 = (f32[48]{0:T(128)S(1)}, f32[48]{0:T(128)}, u32[]{:S(2)}) copy-start(f32[48]{0:T(128)} %param.33) | copy-start | bytes 580
  7.3 10.0 %copy-start.67 = (f32[48]{0:T(128)S(1)}, f32[48]{0:T(128)}, u32[]{:S(2)}) copy-start(f32[48]{0:T(128)} %param.34) | copy-start | bytes 580
  7.3 10.0 %copy-start.68 = (f32[48]{0:T(128)S(1)}, f32[48]{0:T(128)}, u32[]{:S(2)}) copy-start(f32[48]{0:T(128)} %param.35) | copy-start | bytes 580
  7.3 10.0 %copy-start.61 = (f32[192]{0:T(256)S(1)}, f32[192]{0:T(256)}, u32[]{:S(2)}) copy-start(f32[192]{0:T(256)} %param.37) | copy-start | bytes 2308
  7.3 10.0 %copy-start.69 = (f32[48]{0:T(128)S(1)}, f32[48]{0:T(128)}, u32[]{:S(2)}) copy-start(f32[48]{0:T(128)} %param.39) | copy-start | bytes 580
  7.3 10.0 %copy-start.53 = (s32[4]{0:T(128)S(1)}, s32[4]{0:T(128)}, u32[]{:S(2)}) copy-start(s32[4]{0:T(128)} %param.22) | copy-start | bytes 52
  7.3 10.0 %copy-start.54 = (s32[2]{0:T(128)S(1)}, s32[2]{0:T(128)}, u32[]{:S(2)}) copy-start(s32[2]{0:T(128)} %param.23) | copy-start | bytes 28
  7.3 75.9 %all-gather.6.cloned.1.call-start = ((), (), s32[]{:S(2)}) async-start(), calls=%async_computation.5 | async-start | bytes 1671168 | tf_op jit(solution)/shard_map/all_gather | solution.py:267
  9.0 93.4 %all-gather.8.cloned.1.call-start = ((), (), s32[]{:S(2)}) async-start(), calls=%async_computation.6 | async-start | bytes 3760128 | tf_op jit(solution)/shard_map/all_gather | solution.py:270
  10.8 131.9 %all-gather.10.cloned.1.call-start = ((), (), s32[]{:S(2)}) async-start(), calls=%async_computation.7 | async-start | bytes 1253376 | tf_op jit(solution)/shard_map/all_gather | solution.py:273
  12.4 185.3 %all-gather.12.cloned.1.call-start = ((), (), s32[]{:S(2)}) async-start(), calls=%async_computation.8 | async-start | bytes 5013504 | tf_op jit(solution)/shard_map/all_gather | solution.py:277
  14.3 72.1 %copy-start.19 = (bf16[2,256,768]{2,1,0:T(8,128)(2,1)S(1)}, bf16[2,256,768]{2,1,0:T(8,128)(2,1)}, u32[]{:S(2)}) copy-start(bf16[2,256,768]{2,1,0:T(8,128)(2,1)} %param.21) | copy-start | bytes 2359300
  14.3 238.1 %all-gather.14.cloned.1.call-start = ((), (), s32[]{:S(2)}) async-start(), calls=%async_computation.9 | async-start | bytes 5013504 | tf_op jit(solution)/shard_map/all_gather | solution.py:279
  15.2 463.9 %reduce-scatter.10.cloned.1.call-start = ((), (), s32[]{:S(2)}) async-start(), calls=%async_computation.12 | async-start | bytes 2506752 | tf_op jit(solution)/shard_map/reduce_scatter | solution.py:310
  83.2 3.9 copy-start.18
  142.7 3.4 copy-start.4
  142.7 3.4 copy-start.38
  142.7 3.4 copy-start.58
  197.8 8.2 copy-start.11
  197.8 8.2 copy-start.56
  252.5 8.0 copy-start.47
  252.5 8.0 copy-start.55
  260.4 13.7 %copy-start.12 = (f32[512,768]{1,0:T(8,128)S(1)}, f32[512,768]{1,0:T(8,128)}, u32[]{:S(2)}) copy-start(f32[512,768]{1,0:T(8,128)} %copy-done.10) | copy-start | bytes 4718596
  274.1 7.8 copy-start.34
  274.1 7.8 copy-start.70
  274.1 7.8 copy-start.31
  281.9 7.1 copy-start.42
  299.1 3.3 copy-start.26
  310.8 7.5 slice-start
  313.2 5.2 copy-start.24
  313.2 5.2 slice-start.1
  325.8 154.8 %reduce-scatter.6.cloned.1.call-start = ((), (), s32[]{:S(2)}) async-start(), calls=%async_computation.10 | async-start | bytes 3342336 | tf_op jit(solution)/shard_map/reduce_scatter | solution.py:304
  331.3 8.5 %copy-start.46 = (bf16[4,128,3,12,64]{1,0,4,3,2:T(4,128)(2,1)}, bf16[4,128,3,12,64]{1,0,4,3,2:T(4,128)(2,1)S(1)}, u32[]{:S(2)}) copy-start(bf16[4,128,3,12,64]{1,0,4,3,2:T(4,128)(2,1)S(1)} %copy.104) | copy-start | bytes 7077892
  343.5 3.8 copy-start.7
  355.2 195.7 %reduce-scatter.8.cloned.1.call-start = ((), (), s32[]{:S(2)}) async-start(), calls=%async_computation.11 | async-start | bytes 7520256 | tf_op jit(solution)/shard_map/reduce_scatter | solution.py:307
  356.3 3.8 copy-start.33
  365.1 7.1 copy-start.48
  365.1 300.8 %reduce-scatter.14.cloned.1.call-start = ((), (), s32[]{:S(2)}) async-start(), calls=%async_computation.14 | async-start | bytes 10027008 | tf_op jit(solution)/shard_map/reduce_scatter | solution.py:316
  382.3 6.4 copy-start.13
  382.3 399.2 %reduce-scatter.12.cloned.1.call-start = ((), (), s32[]{:S(2)}) async-start(), calls=%async_computation.13 | async-start | bytes 10027008 | tf_op jit(solution)/shard_map/reduce_scatter | solution.py:314
  383.7 5.0 copy-start.35
  394.5 430.5 %all-reduce.24.cloned.1.call-start = ((), (), s32[]{:S(2)}) async-start(), calls=%async_computation.15 | async-start | bytes 1966080 | tf_op jit(solution)/shard_map/psum | solution.py:320
  (36 other events, 61.0 us)
Sparse Core Ops, SparseCore 0:
  11.0 42.4 all-gather.5
  56.4 45.9 all-gather.7
  105.3 37.3 all-gather.9
  145.4 52.3 all-gather.11
  200.5 51.9 all-gather.13
  326.0 61.5 reduce-scatter.9
  391.8 65.5 reduce-scatter.5
  462.0 88.8 reduce-scatter.7
  555.0 110.8 reduce-scatter.13
  670.4 111.0 reduce-scatter.11
  785.8 39.0 all-reduce.23
where the time goes:
time: 845 us; the launch traced here: 840 us
  waiting for transfers between devices  434 us (51%)
  matrix products  159 us (19%)
  blocking collectives  129 us (15%)
  local copies, waits for them, and re-layouts  51.9 us (6%)
  other arithmetic  47.3 us (6%)
  between operations  18 us (2%)
    unnamed x2, blocking collectives  124 us
    reduce_scatter x1, waiting for transfers between devices, shards(): lax.psum_scatter(totals[10], 'fsdp', scatter_dimension=0, tiled=True)  114 us
    reduce_scatter x1, waiting for transfers between devices, shards(): lax.psum_scatter(totals[12], 'fsdp', scatter_dimension=0, tiled=True)  113 us
    reduce_scatter x1, waiting for transfers between devices, shards(): lax.psum_scatter(totals[3], 'fsdp', scatter_dimension=0, tiled=True)  68.6 us
    all_gather x1, waiting for transfers between devices, shards(): lax.all_gather(copies[10], 'fsdp', axis=0, tiled=True)  49.2 us
    dot_general x8, matrix products, against(): lax.dot_general(left, right, (((1,), (1,)), ((), ())), preferred_element_...  44.8 us
    all_gather x1, waiting for transfers between devices, shards(): lax.all_gather(copies[12], 'fsdp', axis=0, tiled=True)  41.5 us
    dot_general x8, matrix products, across_rows(): lax.dot_general(left, right, (((0,), (0,)), ((), ())), preferred_element_...  39.9 us
  transfers between devices with their start and end apart: 11, of which 8 were waited for; matrix products, arithmetic and copies ran while one was open for 19% of the time, Pallas kernels for 0%

commit v1 on v0

--- a/solution.py
+++ b/solution.py
@@ -317,7 +317,7 @@
         lax.psum_scatter(totals[13], "fsdp", scatter_dimension=0, tiled=True),
     )
     reduced = (
-        lax.psum(shares[0].astype(jnp.bfloat16), "rep").astype(jnp.float32),
+        jnp.sum(lax.all_gather(shares[0].astype(jnp.bfloat16), "rep"), axis=0).astype(jnp.float32),
         lax.psum(shares[1].astype(jnp.bfloat16), "rep").astype(jnp.float32),
         lax.psum(shares[2].astype(jnp.bfloat16), "rep").astype(jnp.float32),
         lax.psum(shares[3].astype(jnp.bfloat16), "rep").astype(jnp.float32),

time: 845 us -> 831 us (0.983)
  waiting for transfers between devices: 434 us -> 422 us
    reduce_scatter x1, waiting for transfers between devices: 68.6 us -> 0.01 us  [shards(): lax.psum_scatter(totals[3], 'fsdp', scatter_dimension=0, tiled=True)]
    reduce_scatter x1, waiting for transfers between devices: 0.01 us -> 58.8 us  [shards(): lax.psum_scatter(totals[0], 'fsdp', scatter_dimension=1, tiled=True)]
    unnamed x179 -> x211, local copies, waits for them, and re-layouts: 18 us -> 15.9 us
  transfers between devices with their start and end apart: 11 -> 11, of which waited for: 8 -> 8; matrix products, arithmetic and copies ran while one was open for 19% -> 20% of each run, Pallas kernels for 0% -> 0%
where the time goes in v1:
time: 831 us; the launch traced here: 827 us
  waiting for transfers between devices  422 us (51%)
  matrix products  157 us (19%)
  blocking collectives  136 us (16%)
  local copies, waits for them, and re-layouts  50.4 us (6%)
  other arithmetic  42.4 us (5%)
  between operations  18.8 us (2%)
    unnamed x2, blocking collectives  125 us
    reduce_scatter x1, waiting for transfers between devices, shards(): lax.psum_scatter(totals[10], 'fsdp', scatter_dimension=0, tiled=True)  114 us
    reduce_scatter x1, waiting for transfers between devices, shards(): lax.psum_scatter(totals[12], 'fsdp', scatter_dimension=0, tiled=True)  110 us
    reduce_scatter x1, waiting for transfers between devices, shards(): lax.psum_scatter(totals[0], 'fsdp', scatter_dimension=1, tiled=True)  58.8 us
    all_gather x1, waiting for transfers between devices, shards(): lax.all_gather(copies[10], 'fsdp', axis=0, tiled=True)  49.2 us
    dot_general x8, matrix products, against(): lax.dot_general(left, right, (((1,), (1,)), ((), ())), preferred_element_...  47.4 us
    all_gather x1, waiting for transfers between devices, shards(): lax.all_gather(copies[12], 'fsdp', axis=0, tiled=True)  41 us
    dot_general x8, matrix products, across_rows(): lax.dot_general(left, right, (((0,), (0,)), ((), ())), preferred_element_...  40 us
  transfers between devices with their start and end apart: 11, of which 8 were waited for; matrix products, arithmetic and copies ran while one was open for 20% of the time, Pallas kernels for 0%

profile of v1, /device:TPU:0, one launch (start us, length us, event | category | flops | bytes accessed | tf_op | source)
XLA Modules:
  0.0 826.9 jit_solution(14344076467312730411)
XLA Ops:
  19.3 63.7 %all-reduce.19 = (bf16[768]{0:T(1024)(128)(2,1)S(1)}, bf16[768]{0:T(1024)(128)(2,1)S(1)}, bf16[768]{0:T(1024)(128)(2,1)S(1)}, bf16[768]{0:T(1024)(128)(2,1)S(1)}...) all-reduce(bf16[768]{0:T(1024)(128)(2,1)S(1)} %dynamic-update-slice, ...), channel_id=1, replica_groups=mesh['rep'=2,'fsdp'=16] {'fsdp'}, use_global_device_ids=true, to_apply=%add.4 | all-reduce | flops 9216 | bytes 36864
  83.1 2.0 copy.84
  92.0 10.3 %all-gather.10.cloned.1.call-done = bf16[768,2304]{1,0:T(8,128)(2,1)} async-done(((bf16[48,2304]{1,0:T(8,128)(2,1)}), bf16[768,2304]{1,0:T(8,128)(2,1)}) %all-gather.10.cloned.1.call-update) | async-done | bytes 3538960 | tf_op jit(solution)/shard_map/all_gather | solution.py:270
  102.3 5.4 fusion.16
  107.7 2.8 copy.92
  110.5 2.2 reshape.319
  112.7 4.0 fusion.15
  116.7 2.5 copy.85
  119.2 4.2 reshape.317
  128.5 1.9 fusion.88
  137.5 5.1 all-gather.12.cloned.1.call-done
  142.5 3.1 fusion.91
  148.4 49.2 %all-gather.14.cloned.1.call-done = bf16[768,3072]{1,0:T(8,128)(2,1)} async-done(((bf16[48,3072]{1,0:T(8,128)(2,1)}), bf16[768,3072]{1,0:T(8,128)(2,1)}) %all-gather.14.cloned.1.call-update) | async-done | bytes 4718608 | tf_op jit(solution)/shard_map/all_gather | solution.py:277
  197.6 8.4 %fusion.83 = f32[512,3072]{1,0:T(8,128)} fusion(bf16[768,3072]{1,0:T(8,128)(2,1)} %all-gather.14.cloned.1.call-done, f32[512,768]{1,0:T(8,128)} %copy-done.30, f32[768]{0:T(1024)S(1)} %convert_element_type.379, f32[768]{0:T(1024)S(1)} %convert_element_type.377, f32[512]{0:T(512)S(1)} %add_rsqrt_fusion.2, f32[512]{0:T(512)S(1)} %broadcast_multiply_fusion.10), kind=kOutput, calls=%fused_computation.200 | convolution fusion | flops 2417885184 | bytes 12593152 | tf_op jit(solution)/shard_map/dot_general | solution.py:94
  206.0 5.2 fusion.84
  211.3 41.0 %all-gather.16.cloned.1.call-done = bf16[3072,768]{1,0:T(8,128)(2,1)} async-done(((bf16[192,768]{1,0:T(8,128)(2,1)}), bf16[3072,768]{1,0:T(8,128)(2,1)}) %all-gather.16.cloned.1.call-update) | async-done | bytes 4718608 | tf_op jit(solution)/shard_map/all_gather | solution.py:279
  252.3 8.0 fusion.93
  260.3 13.7 %convert_reduce_fusion = (f32[3072]{0:T(1024)S(1)}, bf16[512,3072]{1,0:T(8,128)(2,1)S(1)}, f32[3072]{0:T(1024)S(1)}, bf16[512,3072]{1,0:T(8,128)(2,1)S(1)}) fusion(f32[512,3072]{1,0:T(8,128)} %fusion.84, f32[3072]{0:T(1024)S(1)} %convert_element_type.383, f32[512,3072]{1,0:T(8,128)} %fusion.93, f32[512,3072]{1,0:T(8,128)} %fusion.83, ...), kind=kOutput, calls=%fused_computation.20 | convolution fusion | flops 2488264704 | bytes 30707712 | tf_op jit(solution)/shard_map/dot_general | solution.py:20
  274.0 7.7 multiply_reduce_fusion.4
  281.8 7.0 convert_reduce_fusion.6
  290.0 2.2 fusion.52
  293.9 2.4 copy.98
  296.3 2.6 reshape.321
  298.9 3.4 fusion.43
  304.6 2.1 multiply_bitcast_fusion.2
  310.7 2.2 reshape.324
  312.9 3.8 convolution_add_fusion.6
  319.1 3.6 copy.104
  322.7 4.9 multiply_reduce_fusion
  332.9 2.5 copy.111
  337.3 2.1 fusion.24
  339.3 5.0 convolution_add_fusion
  345.4 5.9 fusion.85
  351.3 10.2 %convolution_add_fusion.1 = f32[3072,768]{1,0:T(8,128)} fusion(f32[3072,768]{1,0:T(8,128)S(1)} %fusion.85, bf16[512,768]{1,0:T(8,128)(2,1)S(1)} %bitcast.218, f32[512,3072]{1,0:T(8,128)} %fusion.84, f32[3072]{0:T(1024)S(1)} %convert_element_type.383), kind=kOutput, calls=%fused_computation.31 | convolution fusion | flops 2434007040 | bytes 25964544 | tf_op jit(solution)/shard_map/dot_general | solution.py:14
  362.9 5.0 fusion.82
  367.9 5.9 convolution_add_fusion.2
  374.2 4.9 fusion.26
  379.4 3.5 multiply_reduce_fusion.6
  387.6 3.2 convolution_add_fusion.5
  393.3 61.4 %all-reduce.18 = (bf16[768]{0:T(1024)(128)(2,1)S(1)}, bf16[768]{0:T(1024)(128)(2,1)S(1)}, bf16[768]{0:T(1024)(128)(2,1)S(1)}, bf16[768]{0:T(1024)(128)(2,1)S(1)}...) all-reduce(f32[768]{0:T(1024)S(1)} %add.355, ...), channel_id=4, replica_groups=mesh['rep'=2,'fsdp'=16] {'fsdp'}, use_global_device_ids=true, to_apply=%region_28.0.clone | all-reduce | flops 9216 | bytes 55296
  455.3 5.2 all-reduce.20
  465.2 9.1 %add_convert_fusion.5 = bf16[512,768]{1,0:T(8,128)(2,1)} fusion(f32[512,768]{1,0:T(8,128)S(1)} %copy-done.33, bf16[3072,768]{1,0:T(8,128)(2,1)} %all-gather.16.cloned.1.call-done, f32[768]{0:T(1024)S(1)} %convert_element_type.387, f32[512,3072]{1,0:T(8,128)} %fusion.83, f32[3072]{0:T(1024)S(1)} %convert_element_type.383), kind=kOutput, calls=%fused_computation.103 | convolution fusion | flops 2432827392 | bytes 13384704 | tf_op jit(solution)/shard_map/dot_general | solution.py:98
  477.7 109.9 %reduce-scatter.14.cloned.1.call-done = f32[192,768]{1,0:T(8,128)} async-done(((f32[3072,768]{1,0:T(8,128)}), f32[192,768]{1,0:T(8,128)}) %reduce-scatter.14.cloned.1.call-update) | async-done | bytes 589840 | tf_op jit(solution)/shard_map/reduce_scatter | solution.py:316
  589.4 114.0 %reduce-scatter.12.cloned.1.call-done = f32[48,3072]{1,0:T(8,128)} async-done(((f32[768,3072]{1,0:T(8,128)}), f32[48,3072]{1,0:T(8,128)}) %reduce-scatter.12.cloned.1.call-update) | async-done | bytes 589840 | tf_op jit(solution)/shard_map/reduce_scatter | solution.py:314
  705.2 9.0 %add_convert_fusion.2 = bf16[512,768]{1,0:T(8,128)(2,1)} fusion(f32[512,768]{1,0:T(8,128)S(1)} %copy-done.16, bf16[3072,768]{1,0:T(8,128)(2,1)} %all-gather.16.cloned.1.call-done, f32[768]{0:T(1024)S(1)} %convert_element_type.387, f32[512,3072]{1,0:T(8,128)} %fusion.84, f32[3072]{0:T(1024)S(1)} %convert_element_type.383), kind=kOutput, calls=%fused_computation.97 | convolution fusion | flops 2432827392 | bytes 13384704 | tf_op jit(solution)/shard_map/dot_general | solution.py:98
  714.2 58.8 %reduce-scatter.6.cloned.1.call-done = f32[1000,48]{0,1:T(8,128)} async-done(((f32[1000,768]{0,1:T(8,128)}), f32[1000,48]{0,1:T(8,128)}) %reduce-scatter.6.cloned.1.call-update) | async-done | bytes 192016 | tf_op jit(solution)/shard_map/reduce_scatter | solution.py:304
  774.0 5.3 all-gather.1
  780.0 33.3 %all-reduce.24.cloned.1.call-done = (bf16[48,2304]{1,0:T(8,128)(2,1)}, bf16[48,768]{1,0:T(8,128)(2,1)}, bf16[48,3072]{1,0:T(8,128)(2,1)}, bf16[192,768]{1,0:T(8,128)(2,1)}) async-done(((bf16[48,2304]{1,0:T(8,128)(2,1)}, bf16[48,768]{1,0:T(8,128)(2,1)}, bf16[48,3072]{1,0:T(8,128)(2,1)}, bf16[192,768]{1,0:T(8,128)(2,1)}), (bf16[48,2304]{1,0:T(8,128)(2,1)}, bf16[48,768]{1,0:T(8,128)(2,1)}, ...) | async-done | bytes 884752 | tf_op jit(solution)/shard_map/psum | solution.py:323
  (351 shorter events, 79.5 us)
Async XLA Ops:
  7.2 8.0 copy-start.66
  7.2 7.2 copy-start.54
  7.2 9.9 %copy-start.78 = (f32[48]{0:T(128)S(1)}, f32[48]{0:T(128)}, u32[]{:S(2)}) copy-start(f32[48]{0:T(128)} %param.27) | copy-start | bytes 580
  7.2 9.9 %copy-start.79 = (f32[48]{0:T(128)S(1)}, f32[48]{0:T(128)}, u32[]{:S(2)}) copy-start(f32[48]{0:T(128)} %param.28) | copy-start | bytes 580
  7.2 9.9 %copy-start.80 = (f32[48]{0:T(128)S(1)}, f32[48]{0:T(128)}, u32[]{:S(2)}) copy-start(f32[48]{0:T(128)} %param.30) | copy-start | bytes 580
  7.2 9.9 %copy-start.81 = (f32[48]{0:T(128)S(1)}, f32[48]{0:T(128)}, u32[]{:S(2)}) copy-start(f32[48]{0:T(128)} %param.31) | copy-start | bytes 580
  7.3 9.9 %copy-start.82 = (f32[48]{0:T(128)S(1)}, f32[48]{0:T(128)}, u32[]{:S(2)}) copy-start(f32[48]{0:T(128)} %param.33) | copy-start | bytes 580
  7.3 10.0 %copy-start.83 = (f32[48]{0:T(128)S(1)}, f32[48]{0:T(128)}, u32[]{:S(2)}) copy-start(f32[48]{0:T(128)} %param.34) | copy-start | bytes 580
  7.3 10.0 %copy-start.84 = (f32[48]{0:T(128)S(1)}, f32[48]{0:T(128)}, u32[]{:S(2)}) copy-start(f32[48]{0:T(128)} %param.35) | copy-start | bytes 580
  7.3 10.0 %copy-start.77 = (f32[192]{0:T(256)S(1)}, f32[192]{0:T(256)}, u32[]{:S(2)}) copy-start(f32[192]{0:T(256)} %param.37) | copy-start | bytes 2308
  7.3 10.0 %copy-start.85 = (f32[48]{0:T(128)S(1)}, f32[48]{0:T(128)}, u32[]{:S(2)}) copy-start(f32[48]{0:T(128)} %param.39) | copy-start | bytes 580
  7.3 10.0 %copy-start.67 = (s32[4]{0:T(128)S(1)}, s32[4]{0:T(128)}, u32[]{:S(2)}) copy-start(s32[4]{0:T(128)} %param.22) | copy-start | bytes 52
  7.3 10.0 %copy-start.69 = (s32[2]{0:T(128)S(1)}, s32[2]{0:T(128)}, u32[]{:S(2)}) copy-start(s32[2]{0:T(128)} %param.23) | copy-start | bytes 28
  7.3 75.8 %all-gather.8.cloned.1.call-start = ((), (), s32[]{:S(2)}) async-start(), calls=%async_computation.5 | async-start | bytes 1671168 | tf_op jit(solution)/shard_map/all_gather | solution.py:267
  9.0 93.3 %all-gather.10.cloned.1.call-start = ((), (), s32[]{:S(2)}) async-start(), calls=%async_computation.6 | async-start | bytes 3760128 | tf_op jit(solution)/shard_map/all_gather | solution.py:270
  10.8 131.7 %all-gather.12.cloned.1.call-start = ((), (), s32[]{:S(2)}) async-start(), calls=%async_computation.7 | async-start | bytes 1253376 | tf_op jit(solution)/shard_map/all_gather | solution.py:273
  12.4 185.2 %all-gather.14.cloned.1.call-start = ((), (), s32[]{:S(2)}) async-start(), calls=%async_computation.8 | async-start | bytes 5013504 | tf_op jit(solution)/shard_map/all_gather | solution.py:277
  14.3 71.9 %copy-start.22 = (bf16[2,256,768]{2,1,0:T(8,128)(2,1)S(1)}, bf16[2,256,768]{2,1,0:T(8,128)(2,1)}, u32[]{:S(2)}) copy-start(bf16[2,256,768]{2,1,0:T(8,128)(2,1)} %param.21) | copy-start | bytes 2359300
  14.3 238.0 %all-gather.16.cloned.1.call-start = ((), (), s32[]{:S(2)}) async-start(), calls=%async_computation.9 | async-start | bytes 5013504 | tf_op jit(solution)/shard_map/all_gather | solution.py:279
  15.2 459.1 %reduce-scatter.10.cloned.1.call-start = ((), (), s32[]{:S(2)}) async-start(), calls=%async_computation.12 | async-start | bytes 2506752 | tf_op jit(solution)/shard_map/reduce_scatter | solution.py:310
  83.0 7.3 copy-start.55
  197.6 8.4 %copy-start.13 = (f32[512,768]{1,0:T(8,128)S(1)}, f32[512,768]{1,0:T(8,128)}, u32[]{:S(2)}) copy-start(f32[512,768]{1,0:T(8,128)} %copy-done.12) | copy-start | bytes 4718596
  197.6 8.4 %copy-start.72 = (bf16[768,3072]{1,0:T(8,128)(2,1)S(1)}, bf16[768,3072]{1,0:T(8,128)(2,1)}, u32[]{:S(2)}) copy-start(bf16[768,3072]{1,0:T(8,128)(2,1)} %all-gather.14.cloned.1.call-done) | copy-start | bytes 14155780
  252.3 8.0 copy-start.50
  252.3 8.0 copy-start.71
  260.3 13.7 %copy-start.14 = (f32[512,768]{1,0:T(8,128)S(1)}, f32[512,768]{1,0:T(8,128)}, u32[]{:S(2)}) copy-start(f32[512,768]{1,0:T(8,128)} %copy-done.12) | copy-start | bytes 4718596
  274.0 7.8 copy-start.35
  274.0 7.8 copy-start.86
  274.0 7.8 copy-start.31
  281.8 7.1 copy-start.44
  316.8 159.2 %reduce-scatter.8.cloned.1.call-start = ((), (), s32[]{:S(2)}) async-start(), calls=%async_computation.11 | async-start | bytes 7520256 | tf_op jit(solution)/shard_map/reduce_scatter | solution.py:307
  319.1 8.6 %slice-start = ((s8[6291456]{0:T(1024)(128)(4,1)}), s8[4194304]{0:T(1024)(128)(4,1)S(1)}, s32[]{:S(2)}) async-start(s8[6291456]{0:T(1024)(128)(4,1)} %bitcast.201), calls=%async_computation.16 | async-start | bytes 8388608
  344.3 7.0 copy-start.51
  344.3 243.3 %reduce-scatter.14.cloned.1.call-start = ((), (), s32[]{:S(2)}) async-start(), calls=%async_computation.14 | async-start | bytes 10027008 | tf_op jit(solution)/shard_map/reduce_scatter | solution.py:316
  361.5 6.4 copy-start.15
  361.6 341.8 %reduce-scatter.12.cloned.1.call-start = ((), (), s32[]{:S(2)}) async-start(), calls=%async_computation.13 | async-start | bytes 10027008 | tf_op jit(solution)/shard_map/reduce_scatter | solution.py:314
  373.9 5.3 copy-start.2
  373.9 5.3 copy-start.5
  373.9 5.3 copy-start.56
  373.9 5.3 copy-start.58
  373.9 5.3 copy-start.60
  373.9 5.3 copy-start.62
  373.9 5.3 copy-start.64
  373.9 399.1 %reduce-scatter.6.cloned.1.call-start = ((), (), s32[]{:S(2)}) async-start(), calls=%async_computation.10 | async-start | bytes 3342336 | tf_op jit(solution)/shard_map/reduce_scatter | solution.py:304
  374.2 5.3 copy-start.73
  390.8 74.4 %copy-start.33 = (f32[512,768]{1,0:T(8,128)S(1)}, f32[512,768]{1,0:T(8,128)}, u32[]{:S(2)}) copy-start(f32[512,768]{1,0:T(8,128)} %copy-done.30) | copy-start | bytes 4718596
  390.8 422.5 %all-reduce.24.cloned.1.call-start = ((), (), s32[]{:S(2)}) async-start(), calls=%async_computation.15 | async-start | bytes 1769472 | tf_op jit(solution)/shard_map/psum | solution.py:323
  474.3 231.0 %copy-start.16 = (f32[512,768]{1,0:T(8,128)S(1)}, f32[512,768]{1,0:T(8,128)}, u32[]{:S(2)}) copy-start(f32[512,768]{1,0:T(8,128)} %copy-done.12) | copy-start | bytes 4718596
  (52 other events, 120.0 us)
Sparse Core Ops, SparseCore 0:
  11.0 42.5 all-gather.7
  56.5 45.7 all-gather.9
  105.1 37.3 all-gather.11
  145.2 52.3 all-gather.13
  200.3 51.9 all-gather.15
  316.9 61.4 reduce-scatter.9
  383.0 89.6 reduce-scatter.7
  476.7 110.8 reduce-scatter.13
  592.3 111.0 reduce-scatter.11
  707.0 65.9 reduce-scatter.5
  777.3 35.9 all-reduce.23
